TPU v7x, 256 devices: a whole 4x4x8 slice. The times are simulated.
256 devices in a mesh: tm: 16 (over z_lo, x, core), space: 16 (over z_hi, y).
Axes of the slice: x: 4, y: 4, z: 8 (z_hi: 4, z_lo: 2; z = z_hi * 2 + z_lo), core: 2. Of those that a mesh axis runs over, the one named last changes fastest.
Arguments:
- tokens: bfloat16 [1680, 64, 256], P('space', 'tm'), may hold values from -11 to 11
- w_query: bfloat16 [256, 256], replicated, may hold values from -0.375 to 0.375
- w_key: bfloat16 [256, 256], replicated, may hold values from -0.375 to 0.375
- w_value: bfloat16 [256, 256], replicated, may hold values from -0.375 to 0.375
- w_out: bfloat16 [256, 256], replicated, may hold values from -0.375 to 0.375
- mask: int32 [1680, 1680], P('space'), may hold values from 0 to 1, as said below
- decay: float32 [64, 256], P('tm'), may hold values from 0 to 1
- cotangent: float32 [1680, 64, 256], P('space', 'tm'), may hold values from -6 to 6
Outputs:
- grad_tokens: float32 [1680, 64, 256], P('space', 'tm')
- grad_wq: float32 [256, 256], replicated
- grad_wk: float32 [256, 256], replicated
- grad_wv: float32 [256, 256], replicated
- output_weight_gradient: float32 [256, 256], replicated
Inputs may be any that keep to these rules, and one draw needn't show every extreme that they name: `mask`: every token may attend to itself.
All inputs are finite; a program needn't handle non-finite values.
Results may differ from a plain program's by a relative error of at most 0.03.
The roundings to bfloat16 on the way count: a program that leaves them out, or rounds other values in their place, can miss the bound.
Values may be sent and summed in bfloat16 or wider, within the bound.
A program may use at most 128 MiB of HBM per device.

v0:
```python
import math
import jax
import jax.numpy as jnp
from jax import lax
from jax.sharding import PartitionSpec as P

HEADS = 8


def shifted(array, axis, by):
    devices = lax.axis_size(axis)
    pairs = [(i, i + by) for i in range(devices) if 0 <= i + by < devices]
    return lax.ppermute(array, axis, pairs)


def project(rows_flat, weight):
    return jnp.dot(rows_flat, weight, preferred_element_type=jnp.float32).astype(jnp.bfloat16)


def cross(left, right):
    return lax.dot_general(
        left, right, (((0,), (0,)), ((), ())), preferred_element_type=jnp.float32
    )


def back_project(grads_b, weight):
    return lax.dot_general(
        grads_b, weight, (((1,), (1,)), ((), ())), preferred_element_type=jnp.float32
    )


def shards(tokens, w_query, w_key, w_value, w_out, mask, decay, cotangent):
    tok_rows, round_rows, features = tokens.shape
    head_size = features // HEADS
    score_scale = 1.0 / math.sqrt(head_size)
    x_rounds = jnp.swapaxes(tokens, 0, 1)
    flat_rows = x_rounds.reshape(-1, features)
    queries = project(flat_rows, w_query).reshape(round_rows, tok_rows, HEADS, head_size)
    own_keys = project(flat_rows, w_key).reshape(round_rows, tok_rows, features)
    own_values = project(flat_rows, w_value).reshape(round_rows, tok_rows, features)
    all_keys, all_values = (
        lax.all_gather(own_keys, "space", axis=1, tiled=True),
        lax.all_gather(own_values, "space", axis=1, tiled=True),
    )
    random_key_count = all_keys.shape[1]
    all_keys = all_keys.reshape(round_rows, random_key_count, HEADS, head_size)
    all_values = all_values.reshape(round_rows, random_key_count, HEADS, head_size)
    allowed = mask > 0

    def masked_scores(q_round, k_round):
        scores = (
            jnp.einsum("ihe,jhe->hij", q_round, k_round, preferred_element_type=jnp.float32)
            * score_scale
        )
        return jnp.where(allowed[None], scores, -1e30)

    def forward(round_index):
        scores = masked_scores(queries[round_index], all_keys[round_index])
        maxima = jnp.max(scores, axis=2, keepdims=True)
        expons = jnp.exp(scores - maxima)
        totals = jnp.sum(expons, axis=2, keepdims=True)
        probs_b = (expons / totals).astype(jnp.bfloat16)
        stack_result_matrix = jnp.einsum(
            "hij,jhe->ihe", probs_b, all_values[round_index], preferred_element_type=jnp.float32
        )
        return (stack_result_matrix.astype(jnp.bfloat16), maxima, totals)

    attended, maxima, totals = lax.map(forward, jnp.arange(round_rows))
    local_grads = [None] * round_rows
    reach = [None] * round_rows
    local_grads[round_rows - 1] = cotangent[:, round_rows - 1]
    reach[round_rows - 1] = jnp.ones((1, features), jnp.float32)
    for position in range(round_rows - 2, -1, -1):
        local_grads[position] = (
            cotangent[:, position] + decay[position + 1][None] * local_grads[position + 1]
        )
        reach[position] = decay[position + 1][None] * reach[position + 1]
    block_decay = decay[0][None] * reach[0]
    block_update_message = decay[0][None] * local_grads[0]

    def relay(step_index, state):
        incoming, message = state
        incoming = shifted(message.astype(jnp.bfloat16), "tm", -1).astype(message.dtype)
        return (incoming, block_update_message + block_decay * incoming)

    carried, unused = lax.fori_loop(
        0, lax.axis_size("tm"), relay, (jnp.zeros_like(block_update_message), block_update_message)
    )
    grads = jnp.stack(
        [local_grads[position] + reach[position] * carried for position in range(round_rows)],
        axis=0,
    )
    grads_flat = grads.astype(jnp.bfloat16).reshape(-1, features)
    attended_flat = attended.reshape(-1, features)
    output_weight_gradient = cross(attended_flat, grads_flat)
    upstream = (
        back_project(grads_flat, w_out)
        .astype(jnp.bfloat16)
        .reshape(round_rows, tok_rows, HEADS, head_size)
    )
    deltas = jnp.sum(upstream.astype(jnp.float32) * attended.astype(jnp.float32), axis=3)
    deltas = jnp.swapaxes(deltas, 1, 2)[..., None]

    def backward_round(round_index):
        k_round = all_keys[round_index]
        v_round = all_values[round_index]
        q_round = queries[round_index]
        up_round = upstream[round_index]
        scores = masked_scores(q_round, k_round)
        probs = jnp.exp(scores - maxima[round_index]) / totals[round_index]
        slopes = jnp.einsum("ihe,jhe->hij", up_round, v_round, preferred_element_type=jnp.float32)
        score_grads = (probs * (slopes - deltas[round_index])).astype(jnp.bfloat16)
        grad_query = (
            jnp.einsum("hij,jhe->ihe", score_grads, k_round, preferred_element_type=jnp.float32)
            * score_scale
        )
        grad_key = (
            jnp.einsum("hij,ihe->jhe", score_grads, q_round, preferred_element_type=jnp.float32)
            * score_scale
        )
        grad_value = jnp.einsum(
            "hij,ihe->jhe", probs.astype(jnp.bfloat16), up_round, preferred_element_type=jnp.float32
        )
        partials = jnp.concatenate(
            [
                grad_key.reshape(random_key_count, features),
                grad_value.reshape(random_key_count, features),
            ],
            axis=1,
        )
        partials = partials.astype(jnp.bfloat16).astype(jnp.float32)
        return (grad_query.astype(jnp.bfloat16), partials)

    grad_queries, partial_terms = lax.map(backward_round, jnp.arange(round_rows))
    partial_terms = jnp.swapaxes(partial_terms, 0, 1)
    kv_grads = lax.psum_scatter(
        partial_terms.astype(jnp.bfloat16), "space", scatter_dimension=0, tiled=True
    ).astype(jnp.float32)
    kv_grads = jnp.swapaxes(kv_grads, 0, 1)
    grad_keys = kv_grads[..., :features].astype(jnp.bfloat16).reshape(-1, features)
    grad_values = kv_grads[..., features:].astype(jnp.bfloat16).reshape(-1, features)
    grad_q_flat = grad_queries.reshape(-1, features)
    grad_rows = grads.reshape(-1, features) + back_project(grad_q_flat, w_query)
    grad_rows = grad_rows + back_project(grad_keys, w_key) + back_project(grad_values, w_value)
    grad_tokens = jnp.swapaxes(grad_rows.reshape(round_rows, tok_rows, features), 0, 1)
    summed = lax.psum(
        (
            cross(flat_rows, grad_q_flat),
            cross(flat_rows, grad_keys),
            cross(flat_rows, grad_values),
            output_weight_gradient,
        ),
        ("tm", "space"),
    )
    return (grad_tokens, summed[0], summed[1], summed[2], summed[3])


def solution(mesh):
    return jax.shard_map(
        shards,
        mesh=mesh,
        in_specs=(
            P("space", "tm", None),
            P(),
            P(),
            P(),
            P(),
            P("space", None),
            P("tm", None),
            P("space", "tm", None),
        ),
        out_specs=(P("space", "tm", None), P(), P(), P(), P()),
        check_vma=False,
    )
```

profile of v0, /device:TPU:8, one launch (start us, length us, event | category | flops | bytes accessed | tf_op | source)
XLA Modules:
  0.0 1136.6 jit_solution(881701952524546462)
XLA Ops:
  14.5 117.5 %while.38 = (s32[]{:T(128)}, f32[105,256]{1,0:T(8,128)}, bf16[105,256]{1,0:T(8,128)(2,1)S(1)}, f32[1,256]{1,0:T(1,128)S(1)}, f32[105,256]{1,0:T(8,128)S(1)}, /*index=5*/s32[]{:T(128)}) while((s32[]{:T(128)}, f32[105,256]{1,0:T(8,128)}, bf16[105,256]{1,0:T(8,128)(2,1)S(1)}, f32[1,256]{1,0:T(1,128)S(1)}, f32[105,256]{1,0:T(8,128)S(1)}, ...), condition=%wide.region_1.2_spmd, body=%wide.region_0.1_spmd.sunk | while | flops 107522 | bytes 538733 | solution.py:86
  19.6 3.6 collective-permute-done
  25.1 4.2 collective-permute-done
  31.3 4.6 collective-permute-done
  37.8 4.6 collective-permute-done
  44.4 4.2 collective-permute-done
  50.5 4.2 collective-permute-done
  56.7 4.6 collective-permute-done
  63.2 4.6 collective-permute-done
  69.8 4.6 collective-permute-done
  76.3 5.4 collective-permute-done
  83.7 10.1 collective-permute-done
  95.7 10.1 collective-permute-done
  107.8 7.1 collective-permute-done
  116.8 6.3 collective-permute-done
  125.1 6.3 collective-permute-done
  134.7 6.9 copy.82
  141.5 12.3 %all-gather.5.cloned.1.call-done = bf16[4,1680,256]{2,0,1:T(4,128)(2,1)} async-done(((bf16[4,105,256]{2,0,1:T(4,128)(2,1)}), bf16[4,1680,256]{2,0,1:T(4,128)(2,1)}) %all-gather.5.cloned.1.call-update) | async-done | bytes 3440656 | tf_op jit(solution)/shard_map/all_gather | solution.py:43
  153.8 6.9 copy.85
  160.8 39.1 %while.39 = (s32[]{:T(128)}, bf16[4,105,8,32]{1,3,2,0:T(8,128)(2,1)S(1)}, f32[4,8,105,1]{2,1,3,0:T(8,128)S(1)}, f32[4,8,105,1]{2,1,3,0:T(8,128)S(1)}, s32[4]{0:T...) while((s32[]{:T(128)}, ...), condition=%wide.region_5.6_spmd, body=%wide.region_2.5_spmd.sunk | while | flops 197593216 | bytes 20291880 | solution.py:68
  200.2 316.6 %while.40 = (s32[]{:T(128)}, bf16[4,105,8,32]{1,3,2,0:T(8,128)(2,1)S(1)}, bf16[4,1680,512]{2,0,1:T(4,128)(2,1)}, s32[4]{0:T(128)S(1)}, bf16[4,1680,8,32]{1,3,2,0...) while((s32[]{:T(128)}, ...), condition=%wide.region_8.9_spmd, body=%wide.region_7.8_spmd.sunk | while | flops 467658240 | bytes 43092636 | solution.py:134
  212.0 6.3 copy.148
  218.4 61.0 %dynamic_update_slice.29 = bf16[4,1680,512]{2,0,1:T(4,128)(2,1)} dynamic-update-slice(bf16[4,1680,512]{2,0,1:T(4,128)(2,1)} %get-tuple-element.583, bf16[1,1680,512]{2,0,1:T(2,128)(2,1)} %copy.148, s32[]{:T(128)S(6)} %copy.178, s32[]{:T(128)} %constant.35.clone.1..sunk.1, s32[]{:T(128)} %constant.35.clone.1..sunk.1) | dynamic-update-slice | bytes 3440644 | tf_op jit(solution)/shard_map/while/body/jit(dynamic_update_index_in_dim)/dynamic_update_slice | solution.py:134
  281.9 3.4 exponential_divide_fusion.2
  291.2 6.3 copy.148
  297.5 61.0 %dynamic_update_slice.29 = bf16[4,1680,512]{2,0,1:T(4,128)(2,1)} dynamic-update-slice(bf16[4,1680,512]{2,0,1:T(4,128)(2,1)} %get-tuple-element.583, bf16[1,1680,512]{2,0,1:T(2,128)(2,1)} %copy.148, s32[]{:T(128)S(6)} %copy.178, s32[]{:T(128)} %constant.35.clone.1..sunk.1, s32[]{:T(128)} %constant.35.clone.1..sunk.1) | dynamic-update-slice | bytes 3440644 | tf_op jit(solution)/shard_map/while/body/jit(dynamic_update_index_in_dim)/dynamic_update_slice | solution.py:134
  370.3 6.3 copy.148
  376.7 61.0 %dynamic_update_slice.29 = bf16[4,1680,512]{2,0,1:T(4,128)(2,1)} dynamic-update-slice(bf16[4,1680,512]{2,0,1:T(4,128)(2,1)} %get-tuple-element.583, bf16[1,1680,512]{2,0,1:T(2,128)(2,1)} %copy.148, s32[]{:T(128)S(6)} %copy.178, s32[]{:T(128)} %constant.35.clone.1..sunk.1, s32[]{:T(128)} %constant.35.clone.1..sunk.1) | dynamic-update-slice | bytes 3440644 | tf_op jit(solution)/shard_map/while/body/jit(dynamic_update_index_in_dim)/dynamic_update_slice | solution.py:134
  449.5 6.3 copy.148
  455.8 61.0 %dynamic_update_slice.29 = bf16[4,1680,512]{2,0,1:T(4,128)(2,1)} dynamic-update-slice(bf16[4,1680,512]{2,0,1:T(4,128)(2,1)} %get-tuple-element.583, bf16[1,1680,512]{2,0,1:T(2,128)(2,1)} %copy.148, s32[]{:T(128)S(6)} %copy.178, s32[]{:T(128)} %constant.35.clone.1..sunk.1, s32[]{:T(128)} %constant.35.clone.1..sunk.1) | dynamic-update-slice | bytes 3440644 | tf_op jit(solution)/shard_map/while/body/jit(dynamic_update_index_in_dim)/dynamic_update_slice | solution.py:134
  522.2 331.0 %all-reduce.5.cloned.1.call-done = bf16[1680,4,512]{2,1,0:T(4,128)(2,1)} async-done(((bf16[1680,4,512]{2,1,0:T(4,128)(2,1)}), bf16[1680,4,512]{2,1,0:T(4,128)(2,1)}) %all-reduce.5.cloned.1.call-update) | async-done | bytes 6881296
  858.3 264.8 %all-reduce.7.cloned.1.call-done = (f32[256,256]{0,1:T(8,128)}, f32[256,256]{0,1:T(8,128)}, f32[256,256]{0,1:T(8,128)}, f32[256,256]{1,0:T(8,128)}) async-done(((f32[256,256]{0,1:T(8,128)}, f32[256,256]{0,1:T(8,128)}, f32[256,256]{0,1:T(8,128)}, f32[256,256]{1,0:T(8,128)}), (f32[256,256]{0,1:T(8,128)}, f32[256,256]{0,1:T(8,128)}, f32[256,256]{0,1:T(8,128)}, ...) | async-done | bytes 1048592 | tf_op jit(solution)/shard_map/psum | solution.py:146
  (194 shorter events, 126.7 us)
Async XLA Ops:
  7.2 5.5 copy-start
  7.2 7.0 copy-start.16
  7.2 126.6 %copy-start.18 = (bf16[256,256]{1,0:T(8,128)(2,1)S(1)}, bf16[256,256]{1,0:T(8,128)(2,1)}, u32[]{:S(2)}) copy-start(bf16[256,256]{1,0:T(8,128)(2,1)} %param.18) | copy-start | bytes 393220
  7.2 127.5 %all-gather.3.cloned.1.call-start = ((), (), s32[]{:S(2)}) async-start(), calls=%async_computation | async-start | bytes 3655680 | tf_op jit(solution)/shard_map/all_gather | solution.py:42
  8.3 125.9 %copy-start.1 = (bf16[420,256]{1,0:T(8,128)(2,1)}, bf16[420,256]{1,0:T(8,128)(2,1)S(1)}, u32[]{:S(2)}) copy-start(bf16[420,256]{1,0:T(8,128)(2,1)S(1)} %reshape.106) | copy-start | bytes 645124
  10.4 124.1 %copy-start.13 = (s32[105,1680]{1,0:T(8,128)S(1)}, s32[105,1680]{1,0:T(8,128)}, u32[]{:S(2)}) copy-start(s32[105,1680]{1,0:T(8,128)} %param.19) | copy-start | bytes 2116804
  10.5 143.4 %all-gather.5.cloned.1.call-start = ((), (), s32[]{:S(2)}) async-start(), calls=%async_computation.1 | async-start | bytes 3655680 | tf_op jit(solution)/shard_map/all_gather | solution.py:43
  12.6 840.6 %all-reduce.5.cloned.1.call-start = ((), (), s32[]{:S(2)}) async-start(), calls=%async_computation.2 | async-start | bytes 13762560
  14.5 3.1 collective-permute-start
  18.3 4.9 collective-permute-start
  23.9 5.5 collective-permute-start
  30.0 5.9 collective-permute-start
  36.5 5.9 collective-permute-start
  43.1 5.5 collective-permute-start
  49.2 5.5 collective-permute-start
  55.4 5.9 collective-permute-start
  61.9 5.9 collective-permute-start
  68.5 5.9 collective-permute-start
  75.0 6.7 collective-permute-start
  82.4 11.3 collective-permute-start
  94.4 11.4 %collective-permute-start = (bf16[105,256]{1,0:T(8,128)(2,1)S(1)}, bf16[105,256]{1,0:T(8,128)(2,1)S(1)}, u32[]{:S(2)}, u32[]{:S(2)}) collective-permute-start(bf16[105,256]{1,0:T(8,128)(2,1)S(1)} %get-tuple-element.520), channel_id=1, source_target_pairs={{16,0},{32,16},{48,32},{64,48},{80,64},{96,80},{112,96},{128,112},... | collective-permute-start | bytes 161288 | tf_op jit(solution)/shard_map/while/body/eval_jaxpr/ppermute | solution.py:13
  106.5 8.4 collective-permute-start
  115.5 7.6 collective-permute-start
  123.8 7.6 collective-permute-start
  133.0 1.4 copy-start.5
  133.8 26.9 %copy-start.3 = (f32[420,256]{1,0:T(8,128)}, f32[420,256]{1,0:T(8,128)S(1)}, u32[]{:S(2)}) copy-start(f32[420,256]{1,0:T(8,128)S(1)} %reshape.105) | copy-start | bytes 1290244
  516.8 3.2 copy-start.2
  516.8 5.1 copy-start.4
  516.8 337.7 %copy-start.17 = (bf16[105,4,256]{2,1,0:T(4,128)(2,1)S(1)}, bf16[105,4,256]{2,1,0:T(4,128)(2,1)}, u32[]{:S(2)}) copy-start(bf16[105,4,256]{2,1,0:T(4,128)(2,1)} %param.14) | copy-start | bytes 645124
  516.9 339.8 %copy-start.14 = (bf16[256,256]{1,0:T(8,128)(2,1)S(1)}, bf16[256,256]{1,0:T(8,128)(2,1)}, u32[]{:S(2)}) copy-start(bf16[256,256]{1,0:T(8,128)(2,1)} %param.16) | copy-start | bytes 393220
  516.9 606.2 %all-reduce.7.cloned.1.call-start = ((), (), s32[]{:S(2)}) async-start(), calls=%async_computation.3 | async-start | bytes 2097152 | tf_op jit(solution)/shard_map/psum | solution.py:146
  517.9 339.0 %copy-start.15 = (bf16[256,256]{1,0:T(8,128)(2,1)S(1)}, bf16[256,256]{1,0:T(8,128)(2,1)}, u32[]{:S(2)}) copy-start(bf16[256,256]{1,0:T(8,128)(2,1)} %param.17) | copy-start | bytes 393220
  (8 other events, 7.1 us)
Sparse Core Ops, SparseCore 0:
  11.0 71.6 all-gather.2
  85.7 68.0 all-gather.4
  517.0 336.1 all-reduce.4
  860.4 262.5 all-reduce.6
where the time goes:
time: 1160 us; the launch traced here: 1140 us
  waiting for transfers between devices  694 us (60%)
  local copies, waits for them, and re-layouts  304 us (26%)
  matrix products  66.1 us (6%)
  starting transfers between devices  20.8 us (2%)
  other arithmetic  20 us (2%)
  loops' own time  16.1 us (1%)
  between operations  15 us (1%)
    unnamed x5, waiting for transfers between devices  331 us
    dynamic_update_slice x8, local copies, waits for them, and re-layouts, shards(): lax.map(backward_round, jnp.arange(round_rows))  269 us
    psum x1, waiting for transfers between devices, shards(): lax.psum((cross(flat_rows, grad_q_flat), cross(flat_rows, grad_keys), cro...  265 us
    ppermute x16, waiting for transfers between devices, shifted(): return lax.ppermute(array, axis, pairs)  86.3 us
    dot_general x8, matrix products, masked_scores(): jnp.einsum('ihe,jhe->hij', q_round, k_round, preferred_element_type=jnp.f...  23.9 us
  transfers between devices with their start and end apart: 20, of which 19 were waited for; matrix products, arithmetic and copies ran while one was open for 3% of the time, Pallas kernels for 0%

commit v1 on v0

--- a/solution.py
+++ b/solution.py
@@ -144,13 +144,16 @@
     grad_rows = grad_rows + back_project(grad_keys, w_key) + back_project(grad_values, w_value)
     grad_tokens = jnp.swapaxes(grad_rows.reshape(round_rows, tok_rows, features), 0, 1)
     summed = lax.psum(
-        (
-            cross(flat_rows, grad_q_flat),
-            cross(flat_rows, grad_keys),
-            cross(flat_rows, grad_values),
-            output_weight_gradient,
+        lax.psum(
+            (
+                cross(flat_rows, grad_q_flat),
+                cross(flat_rows, grad_keys),
+                cross(flat_rows, grad_values),
+                output_weight_gradient,
+            ),
+            "tm",
         ),
-        ("tm", "space"),
+        "space",
     )
     return (grad_tokens, summed[0], summed[1], summed[2], summed[3])
 

time: 1160 us -> 1190 us (1.026)
  waiting for transfers between devices: 694 us -> 732 us
    psum x0 -> x1, waiting for transfers between devices: none -> 171 us  [shards(): lax.psum(lax.psum((cross(flat_rows, grad_q_flat), cross(flat_rows, grad_k...]
    psum x1, waiting for transfers between devices: 265 us -> 130 us  [shards(): lax.psum((cross(flat_rows, grad_q_flat), cross(flat_rows, grad_keys), cro...]
    unnamed x5 -> x6, waiting for transfers between devices: 331 us -> 332 us
  transfers between devices with their start and end apart: 20 -> 21, of which waited for: 19 -> 20; matrix products, arithmetic and copies ran while one was open for 3% -> 2% of each run, Pallas kernels for 0% -> 0%
where the time goes in v1:
time: 1190 us; the launch traced here: 1170 us
  waiting for transfers between devices  732 us (62%)
  local copies, waits for them, and re-layouts  304 us (26%)
  matrix products  66.4 us (6%)
  starting transfers between devices  20.9 us (2%)
  other arithmetic  20.2 us (2%)
  loops' own time  16.1 us (1%)
  between operations  15 us (1%)
    unnamed x6, waiting for transfers between devices  332 us
    dynamic_update_slice x8, local copies, waits for them, and re-layouts, shards(): lax.map(backward_round, jnp.arange(round_rows))  269 us
    psum x1, waiting for transfers between devices, shards(): lax.psum(lax.psum((cross(flat_rows, grad_q_flat), cross(flat_rows, grad_k...  171 us
    psum x1, waiting for transfers between devices, shards(): lax.psum((cross(flat_rows, grad_q_flat), cross(flat_rows, grad_keys), cro...  130 us
    ppermute x16, waiting for transfers between devices, shifted(): return lax.ppermute(array, axis, pairs)  86.3 us
    dot_general x8, matrix products, masked_scores(): jnp.einsum('ihe,jhe->hij', q_round, k_round, preferred_element_type=jnp.f...  23.9 us
  transfers between devices with their start and end apart: 21, of which 20 were waited for; matrix products, arithmetic and copies ran while one was open for 2% of the time, Pallas kernels for 0%

profile of v1, /device:TPU:8, one launch (start us, length us, event | category | flops | bytes accessed | tf_op | source)
XLA Modules:
  0.0 1173.9 jit_solution(18399996380067718058)
XLA Ops:
  14.5 117.6 %while.38 = (s32[]{:T(128)}, f32[105,256]{1,0:T(8,128)}, bf16[105,256]{1,0:T(8,128)(2,1)S(1)}, f32[1,256]{1,0:T(1,128)S(1)}, f32[105,256]{1,0:T(8,128)S(1)}, /*index=5*/s32[]{:T(128)}) while((s32[]{:T(128)}, f32[105,256]{1,0:T(8,128)}, bf16[105,256]{1,0:T(8,128)(2,1)S(1)}, f32[1,256]{1,0:T(1,128)S(1)}, f32[105,256]{1,0:T(8,128)S(1)}, ...), condition=%wide.region_1.2_spmd, body=%wide.region_0.1_spmd.sunk | while | flops 107522 | bytes 538733 | solution.py:86
  19.6 3.6 collective-permute-done
  25.1 4.2 collective-permute-done
  31.3 4.6 collective-permute-done
  37.8 4.6 collective-permute-done
  44.4 4.2 collective-permute-done
  50.5 4.2 collective-permute-done
  56.7 4.6 collective-permute-done
  63.2 4.6 collective-permute-done
  69.8 4.6 collective-permute-done
  76.3 5.4 collective-permute-done
  83.7 10.0 collective-permute-done
  95.7 10.1 collective-permute-done
  107.8 7.1 collective-permute-done
  116.9 6.2 collective-permute-done
  125.0 6.4 collective-permute-done
  134.7 6.9 copy.82
  141.7 12.1 %all-gather.5.cloned.1.call-done = bf16[4,1680,256]{2,0,1:T(4,128)(2,1)} async-done(((bf16[4,105,256]{2,0,1:T(4,128)(2,1)}), bf16[4,1680,256]{2,0,1:T(4,128)(2,1)}) %all-gather.5.cloned.1.call-update) | async-done | bytes 3440656 | tf_op jit(solution)/shard_map/all_gather | solution.py:43
  153.8 6.8 copy.85
  160.7 39.7 %while.39 = (s32[]{:T(128)}, bf16[4,105,8,32]{1,3,2,0:T(8,128)(2,1)S(1)}, f32[4,8,105,1]{2,1,3,0:T(8,128)S(1)}, f32[4,8,105,1]{2,1,3,0:T(8,128)S(1)}, s32[4]{0:T...) while((s32[]{:T(128)}, ...), condition=%wide.region_5.6_spmd, body=%wide.region_2.5_spmd.sunk | while | flops 197593216 | bytes 20291880 | solution.py:68
  200.7 316.2 %while.40 = (s32[]{:T(128)}, bf16[4,105,8,32]{1,3,2,0:T(8,128)(2,1)S(1)}, bf16[4,1680,512]{2,0,1:T(4,128)(2,1)}, s32[4]{0:T(128)S(1)}, bf16[4,1680,8,32]{1,3,2,0...) while((s32[]{:T(128)}, ...), condition=%wide.region_8.9_spmd, body=%wide.region_7.8_spmd.sunk | while | flops 467658240 | bytes 43092636 | solution.py:134
  212.5 6.3 copy.148
  218.8 60.9 %dynamic_update_slice.29 = bf16[4,1680,512]{2,0,1:T(4,128)(2,1)} dynamic-update-slice(bf16[4,1680,512]{2,0,1:T(4,128)(2,1)} %get-tuple-element.587, bf16[1,1680,512]{2,0,1:T(2,128)(2,1)} %copy.148, s32[]{:T(128)S(6)} %copy.178, s32[]{:T(128)} %constant.35.clone.1..sunk.1, s32[]{:T(128)} %constant.35.clone.1..sunk.1) | dynamic-update-slice | bytes 3440644 | tf_op jit(solution)/shard_map/while/body/jit(dynamic_update_index_in_dim)/dynamic_update_slice | solution.py:134
  291.6 6.3 copy.148
  297.9 60.9 %dynamic_update_slice.29 = bf16[4,1680,512]{2,0,1:T(4,128)(2,1)} dynamic-update-slice(bf16[4,1680,512]{2,0,1:T(4,128)(2,1)} %get-tuple-element.587, bf16[1,1680,512]{2,0,1:T(2,128)(2,1)} %copy.148, s32[]{:T(128)S(6)} %copy.178, s32[]{:T(128)} %constant.35.clone.1..sunk.1, s32[]{:T(128)} %constant.35.clone.1..sunk.1) | dynamic-update-slice | bytes 3440644 | tf_op jit(solution)/shard_map/while/body/jit(dynamic_update_index_in_dim)/dynamic_update_slice | solution.py:134
  370.6 6.3 copy.148
  376.9 60.9 %dynamic_update_slice.29 = bf16[4,1680,512]{2,0,1:T(4,128)(2,1)} dynamic-update-slice(bf16[4,1680,512]{2,0,1:T(4,128)(2,1)} %get-tuple-element.587, bf16[1,1680,512]{2,0,1:T(2,128)(2,1)} %copy.148, s32[]{:T(128)S(6)} %copy.178, s32[]{:T(128)} %constant.35.clone.1..sunk.1, s32[]{:T(128)} %constant.35.clone.1..sunk.1) | dynamic-update-slice | bytes 3440644 | tf_op jit(solution)/shard_map/while/body/jit(dynamic_update_index_in_dim)/dynamic_update_slice | solution.py:134
  449.7 6.3 copy.148
  456.0 60.9 %dynamic_update_slice.29 = bf16[4,1680,512]{2,0,1:T(4,128)(2,1)} dynamic-update-slice(bf16[4,1680,512]{2,0,1:T(4,128)(2,1)} %get-tuple-element.587, bf16[1,1680,512]{2,0,1:T(2,128)(2,1)} %copy.148, s32[]{:T(128)S(6)} %copy.178, s32[]{:T(128)} %constant.35.clone.1..sunk.1, s32[]{:T(128)} %constant.35.clone.1..sunk.1) | dynamic-update-slice | bytes 3440644 | tf_op jit(solution)/shard_map/while/body/jit(dynamic_update_index_in_dim)/dynamic_update_slice | solution.py:134
  522.0 332.0 %all-reduce.7.cloned.1.call-done = bf16[1680,4,512]{2,1,0:T(4,128)(2,1)} async-done(((bf16[1680,4,512]{2,1,0:T(4,128)(2,1)}), bf16[1680,4,512]{2,1,0:T(4,128)(2,1)}) %all-reduce.7.cloned.1.call-update) | async-done | bytes 6881296
  857.4 130.1 %all-reduce.11.cloned.1.call-done = (f32[256,256]{0,1:T(8,128)}, f32[256,256]{0,1:T(8,128)}, f32[256,256]{0,1:T(8,128)}, f32[256,256]{1,0:T(8,128)}) async-done(((f32[256,256]{0,1:T(8,128)}, f32[256,256]{0,1:T(8,128)}, f32[256,256]{0,1:T(8,128)}, f32[256,256]{1,0:T(8,128)}), (f32[256,256]{0,1:T(8,128)}, f32[256,256]{0,1:T(8,128)}, f32[256,256]{0,1:T(8,128)}, ...) | async-done | bytes 1048592 | tf_op jit(solution)/shard_map/psum | solution.py:147
  989.5 170.8 %all-reduce.9.cloned.1.call-done = (f32[256,256]{0,1:T(8,128)}, f32[256,256]{0,1:T(8,128)}, f32[256,256]{0,1:T(8,128)}, f32[256,256]{1,0:T(8,128)}) async-done(((f32[256,256]{0,1:T(8,128)}, f32[256,256]{0,1:T(8,128)}, f32[256,256]{0,1:T(8,128)}, f32[256,256]{1,0:T(8,128)}), (f32[256,256]{0,1:T(8,128)}, f32[256,256]{0,1:T(8,128)}, f32[256,256]{0,1:T(8,128)}, ...) | async-done | bytes 1048592 | tf_op jit(solution)/shard_map/psum | solution.py:146
  (197 shorter events, 130.6 us)
Async XLA Ops:
  7.2 5.5 copy-start
  7.2 7.0 copy-start.16
  7.2 126.7 %copy-start.18 = (bf16[256,256]{1,0:T(8,128)(2,1)S(1)}, bf16[256,256]{1,0:T(8,128)(2,1)}, u32[]{:S(2)}) copy-start(bf16[256,256]{1,0:T(8,128)(2,1)} %param.18) | copy-start | bytes 393220
  7.2 127.5 %all-gather.3.cloned.1.call-start = ((), (), s32[]{:S(2)}) async-start(), calls=%async_computation | async-start | bytes 3655680 | tf_op jit(solution)/shard_map/all_gather | solution.py:42
  8.3 126.0 %copy-start.1 = (bf16[420,256]{1,0:T(8,128)(2,1)}, bf16[420,256]{1,0:T(8,128)(2,1)S(1)}, u32[]{:S(2)}) copy-start(bf16[420,256]{1,0:T(8,128)(2,1)S(1)} %reshape.106) | copy-start | bytes 645124
  10.4 124.2 %copy-start.13 = (s32[105,1680]{1,0:T(8,128)S(1)}, s32[105,1680]{1,0:T(8,128)}, u32[]{:S(2)}) copy-start(s32[105,1680]{1,0:T(8,128)} %param.19) | copy-start | bytes 2116804
  10.5 143.3 %all-gather.5.cloned.1.call-start = ((), (), s32[]{:S(2)}) async-start(), calls=%async_computation.1 | async-start | bytes 3655680 | tf_op jit(solution)/shard_map/all_gather | solution.py:43
  12.6 841.5 %all-reduce.7.cloned.1.call-start = ((), (), s32[]{:S(2)}) async-start(), calls=%async_computation.2 | async-start | bytes 13762560
  14.5 3.1 collective-permute-start
  18.3 4.9 collective-permute-start
  23.9 5.5 collective-permute-start
  30.0 5.9 collective-permute-start
  36.5 5.9 collective-permute-start
  43.1 5.5 collective-permute-start
  49.2 5.5 collective-permute-start
  55.4 5.9 collective-permute-start
  61.9 5.9 collective-permute-start
  68.5 5.9 collective-permute-start
  75.0 6.7 collective-permute-start
  82.4 11.3 collective-permute-start
  94.4 11.4 collective-permute-start
  106.5 8.4 collective-permute-start
  115.6 7.5 collective-permute-start
  123.8 7.7 collective-permute-start
  133.9 26.7 %copy-start.3 = (f32[420,256]{1,0:T(8,128)}, f32[420,256]{1,0:T(8,128)S(1)}, u32[]{:S(2)}) copy-start(f32[420,256]{1,0:T(8,128)S(1)} %reshape.105) | copy-start | bytes 1290244
  516.9 3.3 copy-start.2
  516.9 338.4 %copy-start.17 = (bf16[105,4,256]{2,1,0:T(4,128)(2,1)S(1)}, bf16[105,4,256]{2,1,0:T(4,128)(2,1)}, u32[]{:S(2)}) copy-start(bf16[105,4,256]{2,1,0:T(4,128)(2,1)} %param.14) | copy-start | bytes 645124
  517.0 470.5 %copy-start.4 = (f32[420,256]{1,0:T(8,128)S(1)}, f32[420,256]{1,0:T(8,128)}, u32[]{:S(2)}) copy-start(f32[420,256]{1,0:T(8,128)} %copy-done.3) | copy-start | bytes 1290244
  517.0 470.4 %all-reduce.11.cloned.1.call-start = ((), (), s32[]{:S(2)}) async-start(), calls=%async_computation.4 | async-start | bytes 2097152 | tf_op jit(solution)/shard_map/psum | solution.py:147
  518.0 469.9 %copy-start.14 = (bf16[256,256]{1,0:T(8,128)(2,1)S(1)}, bf16[256,256]{1,0:T(8,128)(2,1)}, u32[]{:S(2)}) copy-start(bf16[256,256]{1,0:T(8,128)(2,1)} %param.16) | copy-start | bytes 393220
  519.5 468.6 %copy-start.15 = (bf16[256,256]{1,0:T(8,128)(2,1)S(1)}, bf16[256,256]{1,0:T(8,128)(2,1)}, u32[]{:S(2)}) copy-start(bf16[256,256]{1,0:T(8,128)(2,1)} %param.17) | copy-start | bytes 393220
  857.3 303.1 %all-reduce.9.cloned.1.call-start = ((), (), s32[]{:S(2)}) async-start(), calls=%async_computation.3 | async-start | bytes 2097152 | tf_op jit(solution)/shard_map/psum | solution.py:146
  (9 other events, 7.9 us)
Sparse Core Ops, SparseCore 0:
  11.0 71.6 all-gather.2
  85.8 67.9 all-gather.4
  517.1 336.9 all-reduce.6
  857.6 129.7 all-reduce.10
  990.1 170.2 all-reduce.8
